TPU v7x, 512 devices: a whole 4x4x16 slice. The times are simulated.
512 devices in a mesh: pair: 16 (over y, z_lo), task: 32 (over z_hi, x, core).
Axes of the slice: x: 4, y: 4, z: 16 (z_hi: 4, z_lo: 4; z = z_hi * 4 + z_lo), core: 2. Of those that a mesh axis runs over, the one named last changes fastest.
Arguments:
- factor_blocks: bfloat16 [64, 1536, 625], P('task', 'pair'), may hold values from -1.25 to 1.25
- amplitudes: bfloat16 [64, 512, 625], P('task', 'pair'), may hold values from -0.15625 to 0.15625
- residual_in: float32 [64, 512, 625], P('task', 'pair'), may hold values from -6 to 6
- task_owners: int32 [512, 3], replicated, may hold values from 0 to 31, all different within a row; in each aligned block of 16 rows (0 to 15, 16 to 31, ...) at most 2 rows name the same one
- task_local: int32 [512, 4], replicated, may hold values from 0 to 1
Outputs:
- residual_out: float32 [64, 512, 625], P('task', 'pair')
Inputs may be any that keep to these rules, and one draw needn't show every extreme that they name: `task_owners`: the three numbers of a row differ; in each aligned block of 16 rows no number appears more than 2 times.
All inputs are finite; a program needn't handle non-finite values.
Results may differ from a plain program's by a relative error of at most 0.012.
Values may be sent and summed in bfloat16 or wider, within the bound.
A program may use at most 64 MiB of HBM per device.

v0:
```python
import jax
import jax.numpy as jnp
from jax import lax
from jax.sharding import PartitionSpec as P

TV = 25


def per_device(factor_blocks, amplitudes, residual_in, task_owners, task_local):
    pair_count = lax.axis_size("pair")
    task_count = lax.axis_size("task")
    helper = lax.axis_index("pair")
    column = lax.axis_index("task")
    blocks_here = factor_blocks.shape[0]
    tile_width = factor_blocks.shape[2]
    owners_all = task_owners.reshape(task_count, pair_count, 3)
    local_all = task_local.reshape(task_count, pair_count, 4)
    my_owners = lax.dynamic_index_in_dim(owners_all, column, 0, keepdims=False)
    my_local = lax.dynamic_index_in_dim(local_all, column, 0, keepdims=False)
    zero_value = jnp.zeros((), factor_blocks.dtype)
    factor_all, amps_all = (
        lax.all_gather(factor_blocks, "task", axis=0, tiled=True),
        lax.all_gather(amplitudes, "task", axis=0, tiled=True),
    )
    global_ids = my_owners * blocks_here + my_local[:, :3]
    factor_send = jnp.stack([factor_all[global_ids[:, 0]], factor_all[global_ids[:, 1]]], axis=0)
    amp_send = amps_all[global_ids[:, 2]][None]
    factor_recv, amp_recv = (
        lax.all_to_all(factor_send, "pair", split_axis=1, concat_axis=1, tiled=True),
        lax.all_to_all(amp_send, "pair", split_axis=1, concat_axis=1, tiled=True),
    )
    row_factor = factor_recv[0].reshape(-1, tile_width)
    col_factor = factor_recv[1].reshape(-1, tile_width)
    amp_block = amp_recv[0].reshape(-1, tile_width)
    integral_tile = lax.dot_general(
        row_factor, col_factor, (((0,), (0,)), ((), ())), preferred_element_type=jnp.float32
    ).astype(jnp.bfloat16)
    ladder = jnp.einsum(
        "icd,acbd->iab",
        amp_block.reshape(-1, TV, TV),
        integral_tile.reshape(TV, TV, TV, TV),
        preferred_element_type=jnp.float32,
    )
    ladder = ladder.astype(jnp.bfloat16).reshape(-1, tile_width)
    onehot = my_local[:, 3][None, :] == jnp.arange(blocks_here, dtype=jnp.int32)[:, None]
    my_target = lax.dynamic_index_in_dim(onehot, helper, 1, keepdims=False)
    partials = jnp.where(my_target[:, None, None], ladder[None], zero_value)
    block_sums = lax.psum_scatter(partials, "pair", scatter_dimension=1, tiled=True).astype(
        jnp.float32
    )
    return residual_in + block_sums


def solution(mesh):
    placed = (P("task", "pair", None), P("task", "pair", None), P("task", "pair", None), P(), P())
    return jax.shard_map(
        per_device, mesh=mesh, in_specs=placed, out_specs=P("task", "pair", None), check_vma=False
    )
```

profile of v0, /device:TPU:2, one launch (start us, length us, event | category | flops | bytes accessed | tf_op | source)
XLA Modules:
  0.0 456.9 jit_solution(9482900807218954983)
XLA Ops:
  6.5 0.7 all-gather.3.cloned.1.call-update
  7.3 0.7 all-gather.5.cloned.1.call-update
  8.0 0.8 reshape.21
  8.8 0.8 reshape.22
  9.7 87.8 %all-gather.3.cloned.1.call-done = bf16[64,32,625]{2,1,0:T(8,128)(2,1)} async-done(((bf16[2,32,625]{2,1,0:T(8,128)(2,1)}), bf16[64,32,625]{2,1,0:T(8,128)(2,1)}) %all-gather.3.cloned.1.call-update) | async-done | bytes 2560016 | tf_op jit(solution)/shard_map/all_gather | solution.py:23
  97.5 3.2 gather_fusion
  100.7 4.9 %all-to-all-start = ((bf16[1,16,32,625]{3,2,0,1:T(8,128)(2,1)}), bf16[1,16,32,625]{3,2,0,1:T(8,128)(2,1)S(1)}, u32[]{:S(2)}, u32[]{:S(2)}) async-start(bf16[1,16,32,625]{3,2,0,1:T(8,128)(2,1)} %bitcast.5), calls=%async_computation | async-start | bytes 1310720 | tf_op jit(solution)/shard_map/all_to_all | solution.py:30
  105.6 122.4 %all-gather.5.cloned.1.call-done = bf16[64,96,625]{2,1,0:T(8,128)(2,1)} async-done(((bf16[2,96,625]{2,1,0:T(8,128)(2,1)}), bf16[64,96,625]{2,1,0:T(8,128)(2,1)}) %all-gather.5.cloned.1.call-update) | async-done | bytes 7680016 | tf_op jit(solution)/shard_map/all_gather | solution.py:22
  228.0 4.1 gather_fusion.1
  232.1 5.4 %gather_fusion.2 = bf16[16,96,625]{2,1,0:T(8,128)(2,1)} fusion(bf16[64,96,625]{2,1,0:T(8,128)(2,1)} %all-gather.5.cloned.1.call-done, s32[1024]{0:T(1024)S(1)} %get-tuple-element.8), kind=kCustom, calls=%fused_computation.2 | custom fusion | bytes 3840064 | tf_op jit(solution)/shard_map/gather | solution.py:26
  237.5 2.1 pad_maximum_fusion
  239.6 2.5 copy.14
  242.1 4.5 all-to-all-start.1
  246.9 0.6 dynamic-slice
  247.5 0.7 compare_bitcast_fusion
  248.2 3.5 copy.13
  251.7 3.5 reshape.51
  255.2 83.2 %all-to-all-done.1 = bf16[2,16,96,625]{3,2,0,1:T(8,128)(2,1)} async-done(((bf16[2,16,96,625]{3,2,0,1:T(8,128)(2,1)}), bf16[2,16,96,625]{3,2,0,1:T(8,128)(2,1)}, u32[]{:S(2)}, u32[]{:S(2)}) %all-to-all-start.1) | async-done | bytes 3840032 | tf_op jit(solution)/shard_map/all_to_all | solution.py:29
  338.3 3.9 bitcast_convert_fusion.1
  342.2 12.5 %reshape.25 = bf16[25,25,25,25]{3,2,1,0:T(8,128)(2,1)} reshape(bf16[625,625]{1,0:T(8,128)(2,1)S(1)} %bitcast_convert_fusion.1) | data formatting | bytes 1562500 | tf_op jit(solution)/shard_map/reshape | solution.py:41
  354.7 3.6 bitcast_convert_fusion
  358.8 1.3 broadcast_select_fusion
  360.1 88.7 %reduce-scatter.2.cloned.1.call-done = bf16[2,32,625]{2,1,0:T(8,128)(2,1)} async-done(((bf16[2,512,625]{2,1,0:T(8,128)(2,1)}), bf16[2,32,625]{2,1,0:T(8,128)(2,1)}) %reduce-scatter.2.cloned.1.call-update) | async-done | bytes 80016 | tf_op jit(solution)/shard_map/reduce_scatter | solution.py:48
  448.8 1.6 convert_add_fusion
  (18 shorter events, 0.9 us)
Async XLA Ops:
  6.5 90.9 %all-gather.3.cloned.1.call-start = ((), (), s32[]{:S(2)}) async-start(), calls=%async_computation.3 | async-start | bytes 2703360 | tf_op jit(solution)/shard_map/all_gather | solution.py:23
  7.3 220.7 %all-gather.5.cloned.1.call-start = ((), (), s32[]{:S(2)}) async-start(), calls=%async_computation.4 | async-start | bytes 8110080 | tf_op jit(solution)/shard_map/all_gather | solution.py:22
  100.7 141.5 %all-to-all-start = ((bf16[1,16,32,625]{3,2,0,1:T(8,128)(2,1)}), bf16[1,16,32,625]{3,2,0,1:T(8,128)(2,1)S(1)}, u32[]{:S(2)}, u32[]{:S(2)}) async-start(bf16[1,16,32,625]{3,2,0,1:T(8,128)(2,1)} %bitcast.5), calls=%async_computation | async-start | bytes 1310720 | tf_op jit(solution)/shard_map/all_to_all | solution.py:30
  242.1 96.2 %all-to-all-start.1 = ((bf16[2,16,96,625]{3,2,0,1:T(8,128)(2,1)}), bf16[2,16,96,625]{3,2,0,1:T(8,128)(2,1)}, u32[]{:S(2)}, u32[]{:S(2)}) async-start(bf16[2,16,96,625]{3,2,0,1:T(8,128)(2,1)} %copy.14), calls=%async_computation.1 | async-start | bytes 7864320 | tf_op jit(solution)/shard_map/all_to_all | solution.py:29
  246.7 202.1 %reduce-scatter.2.cloned.1.call-start = ((), (), s32[]{:S(2)}) async-start(), calls=%async_computation.5 | async-start | bytes 1392640 | tf_op jit(solution)/shard_map/reduce_scatter | solution.py:48
  342.2 12.5 %copy-start = (bf16[512,25,25,1]{0,2,1,3:T(8,128)(2,1)S(1)}, bf16[512,25,25,1]{0,2,1,3:T(8,128)(2,1)}, u32[]{:S(2)}) copy-start(bf16[512,25,25,1]{0,2,1,3:T(8,128)(2,1)} %reshape.51) | copy-start | bytes 1920004
  358.8 90.0 %copy-start.1 = (f32[2,32,625]{2,1,0:T(8,128)S(1)}, f32[2,32,625]{2,1,0:T(8,128)}, u32[]{:S(2)}) copy-start(f32[2,32,625]{2,1,0:T(8,128)} %param.7) | copy-start | bytes 480004
Sparse Core Ops, SparseCore 0:
  10.5 86.9 all-gather.2
  100.6 127.3 all-gather.4
  360.2 88.5 reduce-scatter.1
where the time goes:
time: 457 us
  waiting for transfers between devices  383 us (84%)
  local copies, waits for them, and re-layouts  37.3 us (8%)
  between operations  13.3 us (3%)
  starting transfers between devices  9.73 us (2%)
  matrix products  7.45 us (2%)
  other arithmetic  5.64 us (1%)
    all_gather x1, waiting for transfers between devices, per_device(): lax.all_gather(factor_blocks, 'task', axis=0, tiled=True)  122 us
    reduce_scatter x1, waiting for transfers between devices, per_device(): lax.psum_scatter(partials, 'pair', scatter_dimension=1, tiled=True)  88.7 us
    all_gather x1, waiting for transfers between devices, per_device(): lax.all_gather(amplitudes, 'task', axis=0, tiled=True)  87.8 us
    all_to_all x1, waiting for transfers between devices, per_device(): lax.all_to_all(factor_send, 'pair', split_axis=1, concat_axis=1, tiled=True)  83.2 us
    reshape x1, local copies, waits for them, and re-layouts, per_device(): integral_tile.reshape(TV, TV, TV, TV)  12.5 us
  transfers between devices with their start and end apart: 5, of which 4 were waited for; matrix products, arithmetic and copies ran while one was open for 6% of the time, Pallas kernels for 0%

commit v1 on v0

--- a/solution.py
+++ b/solution.py
@@ -4,6 +4,13 @@
 from jax.sharding import PartitionSpec as P
 
 TV = 25
+
+
+def exchange_gather(block, mesh_axis, dim):
+    size = lax.axis_size(mesh_axis)
+    blocks = jnp.stack([block for _ in range(size)])
+    blocks = lax.all_to_all(blocks, mesh_axis, split_axis=0, concat_axis=0)
+    return jnp.concatenate(blocks, axis=dim)
 
 
 def per_device(factor_blocks, amplitudes, residual_in, task_owners, task_local):
@@ -20,7 +27,7 @@
     zero_value = jnp.zeros((), factor_blocks.dtype)
     factor_all, amps_all = (
         lax.all_gather(factor_blocks, "task", axis=0, tiled=True),
-        lax.all_gather(amplitudes, "task", axis=0, tiled=True),
+        exchange_gather(amplitudes, "task", 0),
     )
     global_ids = my_owners * blocks_here + my_local[:, :3]
     factor_send = jnp.stack([factor_all[global_ids[:, 0]], factor_all[global_ids[:, 1]]], axis=0)

time: 457 us -> 476 us (1.042)
  the two profiles are of different devices: /device:TPU:2 before, /device:TPU:6 now
where the time goes in v1:
time: 476 us; the launch traced here: 475 us
  waiting for transfers between devices  358 us (75%)
  starting transfers between devices  53 us (11%)
  local copies, waits for them, and re-layouts  37 us (8%)
  between operations  13.6 us (3%)
  matrix products  7.46 us (2%)
  other arithmetic  5.64 us (1%)
    all_to_all x1, waiting for transfers between devices, exchange_gather(): blocks = lax.all_to_all(blocks, mesh_axis, split_axis=0, concat_axis=0)  144 us
    reduce_scatter x1, waiting for transfers between devices, per_device(): lax.psum_scatter(partials, 'pair', scatter_dimension=1, tiled=True)  86.5 us
    all_to_all x1, waiting for transfers between devices, per_device(): lax.all_to_all(factor_send, 'pair', split_axis=1, concat_axis=1, tiled=True)  82.9 us
    all_gather x1, waiting for transfers between devices, per_device(): lax.all_gather(factor_blocks, 'task', axis=0, tiled=True)  44.1 us
    all_to_all x1, starting transfers between devices, per_device(): lax.all_to_all(factor_send, 'pair', split_axis=1, concat_axis=1, tiled=True)  25.7 us
    all_to_all x1, starting transfers between devices, exchange_gather(): blocks = lax.all_to_all(blocks, mesh_axis, split_axis=0, concat_axis=0)  18.3 us
    reshape x1, local copies, waits for them, and re-layouts, per_device(): integral_tile.reshape(TV, TV, TV, TV)  12.5 us
  transfers between devices with their start and end apart: 5, of which 4 were waited for; matrix products, arithmetic and copies ran while one was open for 6% of the time, Pallas kernels for 0%

profile of v1, /device:TPU:6, one launch (start us, length us, event | category | flops | bytes accessed | tf_op | source)
XLA Modules:
  0.0 475.1 jit_solution(1518794759411097529)
XLA Ops:
  6.5 0.7 all-gather.2.cloned.1.call-update
  7.3 2.8 stack.8
  10.1 18.3 %all-to-all-start = ((bf16[32,2,32,625]{3,2,1,0:T(8,128)(2,1)}), bf16[32,2,32,625]{3,2,1,0:T(8,128)(2,1)S(1)}, u32[]{:S(2)}, u32[]{:S(2)}) async-start(bf16[32,2,32,625]{3,2,1,0:T(8,128)(2,1)} %stack.8), calls=%async_computation | async-start | bytes 5242880 | tf_op jit(solution)/shard_map/all_to_all | solution.py:12
  28.7 144.1 %all-to-all-done = bf16[32,2,32,625]{3,2,1,0:T(8,128)(2,1)S(1)} async-done(((bf16[32,2,32,625]{3,2,1,0:T(8,128)(2,1)}), bf16[32,2,32,625]{3,2,1,0:T(8,128)(2,1)S(1)}, u32[]{:S(2)}, u32[]{:S(2)}) %all-to-all-start) | async-done | bytes 2560032 | tf_op jit(solution)/shard_map/all_to_all | solution.py:12
  172.8 1.5 gather_fusion
  174.3 8.8 %all-to-all-start.1 = ((bf16[1,16,32,625]{3,2,0,1:T(8,128)(2,1)}), bf16[1,16,32,625]{3,2,0,1:T(8,128)(2,1)S(1)}, u32[]{:S(2)}, u32[]{:S(2)}) async-start(bf16[1,16,32,625]{3,2,0,1:T(8,128)(2,1)} %bitcast.6), calls=%async_computation.1 | async-start | bytes 1310720 | tf_op jit(solution)/shard_map/all_to_all | solution.py:37
  183.1 44.1 %all-gather.2.cloned.1.call-done = bf16[64,96,625]{2,1,0:T(8,128)(2,1)} async-done(((bf16[2,96,625]{2,1,0:T(8,128)(2,1)}), bf16[64,96,625]{2,1,0:T(8,128)(2,1)}) %all-gather.2.cloned.1.call-update) | async-done | bytes 7680016 | tf_op jit(solution)/shard_map/all_gather | solution.py:29
  227.2 4.1 gather_fusion.2
  231.3 5.4 %gather_fusion.1 = bf16[16,96,625]{2,1,0:T(8,128)(2,1)} fusion(bf16[64,96,625]{2,1,0:T(8,128)(2,1)} %all-gather.2.cloned.1.call-done, s32[1024]{0:T(1024)S(1)} %get-tuple-element.9), kind=kCustom, calls=%fused_computation.1 | custom fusion | bytes 3840064 | tf_op jit(solution)/shard_map/gather | solution.py:33
  236.7 2.1 pad_maximum_fusion
  238.8 2.5 copy.13
  241.3 25.7 %all-to-all-start.2 = ((bf16[2,16,96,625]{3,2,0,1:T(8,128)(2,1)}), bf16[2,16,96,625]{3,2,0,1:T(8,128)(2,1)}, u32[]{:S(2)}, u32[]{:S(2)}) async-start(bf16[2,16,96,625]{3,2,0,1:T(8,128)(2,1)} %copy.13), calls=%async_computation.2 | async-start | bytes 7864320 | tf_op jit(solution)/shard_map/all_to_all | solution.py:36
  267.2 0.6 dynamic-slice
  267.8 0.7 compare_bitcast_fusion
  268.5 3.5 copy.12
  272.0 3.5 reshape.57
  275.5 82.9 %all-to-all-done.2 = bf16[2,16,96,625]{3,2,0,1:T(8,128)(2,1)} async-done(((bf16[2,16,96,625]{3,2,0,1:T(8,128)(2,1)}), bf16[2,16,96,625]{3,2,0,1:T(8,128)(2,1)}, u32[]{:S(2)}, u32[]{:S(2)}) %all-to-all-start.2) | async-done | bytes 3840032 | tf_op jit(solution)/shard_map/all_to_all | solution.py:36
  358.4 3.9 bitcast_convert_fusion.1
  362.2 12.5 %reshape.31 = bf16[25,25,25,25]{3,2,1,0:T(8,128)(2,1)} reshape(bf16[625,625]{1,0:T(8,128)(2,1)S(1)} %bitcast_convert_fusion.1) | data formatting | bytes 1562500 | tf_op jit(solution)/shard_map/reshape | solution.py:48
  374.7 3.6 bitcast_convert_fusion
  378.5 0.3 copy.16
  378.8 1.3 broadcast_select_fusion
  380.1 86.5 %reduce-scatter.2.cloned.1.call-done = bf16[2,32,625]{2,1,0:T(8,128)(2,1)} async-done(((bf16[2,512,625]{2,1,0:T(8,128)(2,1)}), bf16[2,32,625]{2,1,0:T(8,128)(2,1)}) %reduce-scatter.2.cloned.1.call-update) | async-done | bytes 80016 | tf_op jit(solution)/shard_map/reduce_scatter | solution.py:55
  466.7 1.6 convert_add_fusion
  (22 shorter events, 0.7 us)
Async XLA Ops:
  6.5 220.6 %all-gather.2.cloned.1.call-start = ((), (), s32[]{:S(2)}) async-start(), calls=%async_computation.4 | async-start | bytes 8110080 | tf_op jit(solution)/shard_map/all_gather | solution.py:29
  10.1 18.3 %copy-start.2 = (s32[512,4]{0,1:T(4,128)S(1)}, s32[512,4]{0,1:T(4,128)}, u32[]{:S(2)}) copy-start(s32[512,4]{0,1:T(4,128)} %param.9) | copy-start | bytes 24580
  10.1 18.4 %copy-start.3 = (s32[512,3]{0,1:T(4,128)S(1)}, s32[512,3]{0,1:T(4,128)}, u32[]{:S(2)}) copy-start(s32[512,3]{0,1:T(4,128)} %param.8) | copy-start | bytes 18436
  10.1 162.7 %all-to-all-start = ((bf16[32,2,32,625]{3,2,1,0:T(8,128)(2,1)}), bf16[32,2,32,625]{3,2,1,0:T(8,128)(2,1)S(1)}, u32[]{:S(2)}, u32[]{:S(2)}) async-start(bf16[32,2,32,625]{3,2,1,0:T(8,128)(2,1)} %stack.8), calls=%async_computation | async-start | bytes 5242880 | tf_op jit(solution)/shard_map/all_to_all | solution.py:12
  174.3 67.0 %all-to-all-start.1 = ((bf16[1,16,32,625]{3,2,0,1:T(8,128)(2,1)}), bf16[1,16,32,625]{3,2,0,1:T(8,128)(2,1)S(1)}, u32[]{:S(2)}, u32[]{:S(2)}) async-start(bf16[1,16,32,625]{3,2,0,1:T(8,128)(2,1)} %bitcast.6), calls=%async_computation.1 | async-start | bytes 1310720 | tf_op jit(solution)/shard_map/all_to_all | solution.py:37
  241.3 117.1 %all-to-all-start.2 = ((bf16[2,16,96,625]{3,2,0,1:T(8,128)(2,1)}), bf16[2,16,96,625]{3,2,0,1:T(8,128)(2,1)}, u32[]{:S(2)}, u32[]{:S(2)}) async-start(bf16[2,16,96,625]{3,2,0,1:T(8,128)(2,1)} %copy.13), calls=%async_computation.2 | async-start | bytes 7864320 | tf_op jit(solution)/shard_map/all_to_all | solution.py:36
  267.0 199.7 %reduce-scatter.2.cloned.1.call-start = ((), (), s32[]{:S(2)}) async-start(), calls=%async_computation.5 | async-start | bytes 1392640 | tf_op jit(solution)/shard_map/reduce_scatter | solution.py:55
  362.2 12.5 %copy-start = (bf16[512,25,25,1]{0,2,1,3:T(8,128)(2,1)S(1)}, bf16[512,25,25,1]{0,2,1,3:T(8,128)(2,1)}, u32[]{:S(2)}) copy-start(bf16[512,25,25,1]{0,2,1,3:T(8,128)(2,1)} %reshape.57) | copy-start | bytes 1920004
  378.5 88.1 %copy-start.1 = (f32[2,32,625]{2,1,0:T(8,128)S(1)}, f32[2,32,625]{2,1,0:T(8,128)}, u32[]{:S(2)}) copy-start(f32[2,32,625]{2,1,0:T(8,128)} %param.7) | copy-start | bytes 480004
Sparse Core Ops, SparseCore 0:
  10.5 216.6 all-gather.1
  380.2 86.3 reduce-scatter.1
